TPU v7x, 256 devices: a whole 4x4x8 slice. The times are simulated.
256 devices in a mesh: rows: 4 (over z_hi), cols: 64 (over y, z_lo, x, core).
Axes of the slice: x: 4, y: 4, z: 8 (z_hi: 4, z_lo: 2; z = z_hi * 2 + z_lo), core: 2. Of those that a mesh axis runs over, the one named last changes fastest.
Arguments:
- slab: bfloat16 [8192, 65536], P('rows', 'cols'), may hold values from -6 to 6
- transforms: bfloat16 [64, 16384, 512], P('cols', 'rows'), may hold values from -0.25 to 0.25
- owners: int32 [2, 4], replicated, may hold values from 0 to 63, as said below
Outputs:
- updated: bfloat16 [8192, 65536], P('rows', 'cols')
Inputs may be any that keep to these rules, and one draw needn't show every extreme that they name: For each row block, the owners of different rounds differ.
All inputs are finite; a program needn't handle non-finite values.
Results may differ from a plain program's by a relative error of at most 0.0063.
Values may be sent and summed in bfloat16 or wider, within the bound.
A program may use at most 64 MiB of HBM per device.

v0:
```python
import jax
import jax.numpy as jnp
from jax import lax
from jax.sharding import PartitionSpec as P


def spread(block, axis, owner):
    block = jnp.where(lax.axis_index(axis) == owner, block, jnp.zeros_like(block))
    return lax.psum(block, axis)


def shifted(value, axis, steps):
    count = lax.axis_size(axis)
    initial, last = (max(0, -steps), min(count, count - steps))
    return lax.ppermute(value, axis, [(source, source + steps) for source in range(initial, last)])


def apply_windows(transform_set, block_rows):
    product = jnp.einsum(
        "nab,nac->nbc", transform_set, block_rows, preferred_element_type=jnp.float32
    )
    return product.astype(jnp.bfloat16)


def local(slab, transforms, owners):
    row_block = lax.axis_index("rows")
    last_block = lax.axis_size("rows") - 1
    window = transforms.shape[2]
    own_slot = transforms[0]
    wins_count = own_slot.shape[0] // (2 * window)
    local_rows, local_cols = slab.shape
    border = window // 2
    matrix = slab
    for round_index in range(owners.shape[0]):
        owner = owners[round_index][row_block]
        received = spread(own_slot, "cols", owner).reshape(2, wins_count, window, window)
        matrix = apply_windows(received[0], matrix.reshape(wins_count, window, local_cols)).reshape(
            local_rows, local_cols
        )
        below = shifted(matrix[:border], "rows", -1)
        extended = jnp.concatenate([matrix[border:], below], 0).reshape(
            wins_count, window, local_cols
        )
        mixed = apply_windows(received[1], extended)
        final_window = jnp.where(
            row_block == last_block, extended[wins_count - 1], mixed[wins_count - 1]
        )
        mixed = jnp.concatenate([mixed[: wins_count - 1], final_window[None]], 0)
        flat = mixed.reshape(local_rows, local_cols)
        returned = shifted(flat[local_rows - border :], "rows", 1)
        top_rows = jnp.where(row_block == 0, matrix[:border], returned)
        matrix = jnp.concatenate([top_rows, flat[: local_rows - border]], 0)
    return matrix


def solution(mesh):
    return jax.shard_map(
        local,
        mesh=mesh,
        in_specs=(P("rows", "cols"), P("cols", "rows", None), P()),
        out_specs=P("rows", "cols"),
        check_vma=False,
    )
```

profile of v0, /device:TPU:126, one launch (start us, length us, event | category | flops | bytes accessed | tf_op | source)
XLA Modules:
  0.0 693.2 jit_solution(15096287348135712689)
XLA Ops:
  6.5 0.8 fusion.8
  7.3 0.6 constant_dynamic-slice_fusion
  9.2 6.1 select_bitcast_fusion
  15.3 579.8 %all-reduce.3.cloned.1.call-done = (bf16[4096,512]{1,0:T(8,128)(2,1)}, bf16[4096,512]{1,0:T(8,128)(2,1)}) async-done(((bf16[4096,512]{1,0:T(8,128)(2,1)}, bf16[4096,512]{1,0:T(8,128)(2,1)}), (bf16[4096,512]{1,0:T(8,128)(2,1)}, bf16[4096,512]{1,0:T(8,128)(2,1)})) %all-reduce.3.cloned.1.call-update) | async-done | bytes 8388624 | tf_op jit(solution)/shard_map/psum | solution.py:9
  595.1 2.7 fusion.7
  597.8 0.8 copy-done.2
  598.6 2.4 convolution_convert_fusion.3
  601.0 2.0 copy-done
  603.1 2.3 collective-permute-start
  605.4 2.4 slice.92
  607.8 13.3 %collective-permute-done = bf16[256,1024]{1,0:T(8,128)(2,1)S(1)} collective-permute-done((bf16[256,1024]{1,0:T(8,128)(2,1)S(1)}, bf16[256,1024]{1,0:T(8,128)(2,1)S(1)}, u32[]{:S(2)}, u32[]{:S(2)}) %collective-permute-start) | collective-permute-done | bytes 524320 | tf_op jit(solution)/shard_map/ppermute | solution.py:15
  621.1 0.5 pad_maximum_fusion
  621.6 2.4 convolution_convert_fusion.2
  625.2 3.8 collective-permute-start.1
  629.7 12.9 %collective-permute-done.1 = bf16[256,1024]{1,0:T(8,128)(2,1)S(1)} collective-permute-done((bf16[256,1024]{1,0:T(8,128)(2,1)S(1)}, bf16[256,1024]{1,0:T(8,128)(2,1)S(1)}, u32[]{:S(2)}, u32[]{:S(2)}) %collective-permute-start.1) | collective-permute-done | bytes 524320 | tf_op jit(solution)/shard_map/ppermute | solution.py:15
  642.7 1.1 broadcast_select_fusion.1
  643.8 0.5 pad_maximum_fusion.3
  644.2 2.4 convolution_convert_fusion.1
  646.7 2.1 collective-permute-start.2
  649.2 15.0 %collective-permute-done.2 = bf16[256,1024]{1,0:T(8,128)(2,1)S(1)} collective-permute-done((bf16[256,1024]{1,0:T(8,128)(2,1)S(1)}, bf16[256,1024]{1,0:T(8,128)(2,1)S(1)}, u32[]{:S(2)}, u32[]{:S(2)}) %collective-permute-start.2) | collective-permute-done | bytes 524320 | tf_op jit(solution)/shard_map/ppermute | solution.py:15
  664.7 2.4 convolution_convert_fusion
  668.3 3.5 collective-permute-start.3
  672.2 11.5 %collective-permute-done.3 = bf16[256,1024]{1,0:T(8,128)(2,1)S(1)} collective-permute-done((bf16[256,1024]{1,0:T(8,128)(2,1)S(1)}, bf16[256,1024]{1,0:T(8,128)(2,1)S(1)}, u32[]{:S(2)}, u32[]{:S(2)}) %collective-permute-start.3) | collective-permute-done | bytes 524320 | tf_op jit(solution)/shard_map/ppermute | solution.py:15
  683.8 2.5 pad_maximum_fusion.5
  (22 shorter events, 4.2 us)
Async XLA Ops:
  6.5 588.6 %all-reduce.3.cloned.1.call-start = ((), (), s32[]{:S(2)}) async-start(), calls=%async_computation | async-start | bytes 16777216 | tf_op jit(solution)/shard_map/psum | solution.py:9
  595.1 3.4 copy-start.2
  601.0 2.0 copy-start
  603.1 18.1 %collective-permute-start = (bf16[256,1024]{1,0:T(8,128)(2,1)S(1)}, bf16[256,1024]{1,0:T(8,128)(2,1)S(1)}, u32[]{:S(2)}, u32[]{:S(2)}) collective-permute-start(bf16[256,1024]{1,0:T(8,128)(2,1)S(1)} %slice.90), channel_id=1, source_target_pairs={{64,0},{128,64},{192,128},{65,1},{129,65},{193,129},{66,2},{130,66... | collective-permute-start | bytes 1572872 | tf_op jit(solution)/shard_map/ppermute | solution.py:15
  624.8 4.3 copy-start.1
  625.2 17.4 %collective-permute-start.1 = (bf16[256,1024]{1,0:T(8,128)(2,1)S(1)}, bf16[256,1024]{1,0:T(8,128)(2,1)S(1)}, u32[]{:S(2)}, u32[]{:S(2)}) collective-permute-start(bf16[256,1024]{1,0:T(8,128)(2,1)S(1)} %slice.97), channel_id=1, source_target_pairs={{0,64},{64,128},{128,192},{1,65},{65,129},{129,193},{2,66},{66,130... | collective-permute-start | bytes 1572872 | tf_op jit(solution)/shard_map/ppermute | solution.py:15
  646.7 17.5 %collective-permute-start.2 = (bf16[256,1024]{1,0:T(8,128)(2,1)S(1)}, bf16[256,1024]{1,0:T(8,128)(2,1)S(1)}, u32[]{:S(2)}, u32[]{:S(2)}) collective-permute-start(bf16[256,1024]{1,0:T(8,128)(2,1)S(1)} %slice.99), channel_id=1, source_target_pairs={{64,0},{128,64},{192,128},{65,1},{129,65},{193,129},{66,2},{130,66... | collective-permute-start | bytes 1572872 | tf_op jit(solution)/shard_map/ppermute | solution.py:15
  668.3 15.5 %collective-permute-start.3 = (bf16[256,1024]{1,0:T(8,128)(2,1)S(1)}, bf16[256,1024]{1,0:T(8,128)(2,1)S(1)}, u32[]{:S(2)}, u32[]{:S(2)}) collective-permute-start(bf16[256,1024]{1,0:T(8,128)(2,1)S(1)} %slice.106), channel_id=1, source_target_pairs={{0,64},{64,128},{128,192},{1,65},{65,129},{129,193},{2,66},{66,130... | collective-permute-start | bytes 1572872 | tf_op jit(solution)/shard_map/ppermute | solution.py:15
Sparse Core Ops, SparseCore 0:
  15.4 579.6 all-reduce.2
where the time goes:
time: 693 us
  waiting for transfers between devices  633 us (91%)
  between operations  14.9 us (2%)
  other arithmetic  12.7 us (2%)
  starting transfers between devices  11.8 us (2%)
  local copies, waits for them, and re-layouts  11.4 us (2%)
  matrix products  9.72 us (1%)
    psum x1, waiting for transfers between devices, spread(): return lax.psum(block, axis)  580 us
    ppermute x4, waiting for transfers between devices, shifted(): lax.ppermute(value, axis, [(source, source + steps) for source in range(i...  52.8 us
  transfers between devices with their start and end apart: 5, of which 5 were waited for; matrix products, arithmetic and copies ran while one was open for 1% of the time, Pallas kernels for 0%

commit v1 on v0

v1 whole, which is shorter than its diff:
```python
import functools

import jax
import jax.numpy as jnp
from jax import lax
from jax.experimental import pallas as pl
from jax.experimental.pallas import tpu as pltpu
from jax.sharding import PartitionSpec as P

MESH = pl.DeviceIdType.MESH

PARENT = (
    0, 10234, 10234, 10324, 21034, 40231, 40231, 4321,
    10324, 43102, 40123, 34201, 1423, 30421, 30412, 13042,
    10324, 30124, 42310, 31240, 1342, 21043, 24301, 43102,
    1324, 24310, 42130, 21034, 13042, 40213, 20314, 12430,
)
DEPTH = (
    11111, 13333, 22464, 31555, 53531, 24442, 33553, 62664,
    55133, 44266, 55355, 44646, 44242, 35353, 44466, 53355,
    66224, 55335, 64446, 55555, 55333, 46644, 55555, 64644,
    35313, 26426, 53555, 44464, 66622, 35535, 44646, 53553,
)
OPPOSITE = (1, 0, 3, 2, 4)
LINKS = 5
LAG = 5
CHUNKS = 128
SEQS = 26
STEPS = SEQS + LAG * 5
G = 16
BANDS = 8
BAND = 128
W = 512
EDGE = 256
EARLY = 3 + LAG * 5


def digits(words):
    return [[word // 10 ** (4 - i) % 10 for i in range(5)] for word in words]


def tree_tables():
    parent = digits(PARENT)
    depth = digits(DEPTH)
    forward = []
    for place in range(32):
        y, z, x = place // 8, place // 4 % 2, place % 4
        ahead = (
            (y * 2 + z) * 4 + (x + 1) % 4,
            (y * 2 + z) * 4 + (x + 3) % 4,
            ((y + 1) % 4 * 2 + z) * 4 + x,
            ((y + 3) % 4 * 2 + z) * 4 + x,
            (y * 2 + 1 - z) * 4 + x,
        )
        row = []
        for link in range(LINKS):
            source = 0
            if place and ahead[link]:
                tree = parent[ahead[link]].index(OPPOSITE[link])
                source = parent[place][tree]
            row.append(source)
        forward.append(row)
    flat = []
    for place in range(32):
        flat += forward[place] + parent[place] + [level - 1 for level in depth[place]]
    return jnp.array(flat, jnp.int32)


def sweep_kernel(
    owners, table, slot_hbm, slab_hbm, out_hbm,
    own, other, recv, mirror, stage, q, w, below, top, back,
    load_sem, part_send, part_recv, send_sem, recv_sem, mirror_send, mirror_recv,
    up_send, up_recv, down_send, down_recv, out_sem,
):
    row = lax.axis_index("rows")
    col = lax.axis_index("cols")
    core = col % 2
    x = (col // 2) % 4
    z = (col // 8) % 2
    y = col // 16

    def device(yy, zz, xx, cc):
        return {"cols": ((yy * 2 + zz) * 4 + xx) * 2 + cc}

    peers = (
        device(y, z, (x + 1) % 4, core),
        device(y, z, (x + 3) % 4, core),
        device((y + 1) % 4, z, x, core),
        device((y + 3) % 4, z, x, core),
        device(y, 1 - z, x, core),
    )
    partner = device(y, z, x, 1 - core)
    upper = {"rows": (row + 3) % 4}
    lower = {"rows": (row + 1) % 4}

    load = pltpu.make_async_copy(slot_hbm, own, load_sem.at[0])
    load.start()
    load_slab = pltpu.make_async_copy(slab_hbm, w, load_sem.at[1])
    load_slab.start()
    barrier = pltpu.get_barrier_semaphore()
    for peer in peers + (partner, upper, lower):
        pl.semaphore_signal(barrier, inc=1, device_id=peer, device_id_type=MESH)
    pl.semaphore_wait(barrier, 8)

    def part(index, first, count, half):
        return pltpu.make_async_remote_copy(
            src_ref=slot_hbm.at[pl.ds(first, count), half],
            dst_ref=other.at[pl.ds(first, count), half],
            send_sem=part_send.at[index],
            recv_sem=part_recv.at[index],
            device_id=partner,
            device_id_type=MESH,
        )

    parts = (part(0, 0, 32, 1 - core), part(1, 32, 96, 1 - core), part(2, 0, 128, core))
    for copy in parts:
        copy.start()

    place, rooted, root_core = [], [], []
    for k in range(2):
        owner = owners[k, row]
        oy, oz, ox, oc = owner // 16, (owner // 8) % 2, (owner // 2) % 4, owner % 2
        where = (((y + 4 - oy) % 4) * 2 + (z + 2 - oz) % 2) * 4 + (x + 4 - ox) % 4
        place.append(where)
        rooted.append(where == 0)
        root_core.append(oc == core)
    source = [[table[place[k] * 15 + l] for l in range(LINKS)] for k in range(2)]
    entry = [[table[place[k] * 15 + 5 + l] for l in range(LINKS)] for k in range(2)]
    level = [[table[place[k] * 15 + 10 + l] for l in range(LINKS)] for k in range(2)]

    def fill(step, local, passed):
        for l in range(LINKS):
            chunk = None
            if local:
                chunk = step * LINKS + l
                if isinstance(chunk, int):
                    chunk = min(chunk, CHUNKS - 1)
                mine, theirs = own[chunk, core], other[chunk, core]
            for k in range(2):
                value = None
                if passed:
                    value = recv[step - LAG, 0, k]
                    for m in range(1, LINKS):
                        value = jnp.where(source[k][l] == m, recv[step - LAG, m, k], value)
                if local:
                    first = jnp.where(root_core[k], mine, theirs)
                    value = first if value is None else jnp.where(rooted[k], first, value)
                stage[step, l, k] = value

    def send(step):
        for l in range(LINKS):
            pltpu.make_async_remote_copy(
                src_ref=stage.at[step, l],
                dst_ref=recv.at[step, OPPOSITE[l]],
                send_sem=send_sem.at[step],
                recv_sem=recv_sem.at[step],
                device_id=peers[l],
                device_id_type=MESH,
            ).start()

    def whole(ref, step, sem):
        return pltpu.make_async_copy(ref.at[step], ref.at[step], sem.at[step])

    def reflect(step):
        return pltpu.make_async_remote_copy(
            src_ref=recv.at[step],
            dst_ref=mirror.at[step],
            send_sem=mirror_send.at[step],
            recv_sem=mirror_recv.at[step],
            device_id=partner,
            device_id_type=MESH,
        )

    def arrive(step):
        whole(recv, step, recv_sem).wait()
        reflect(step).start()

    def pass_on(step, carry):
        arrive(step - LAG)
        fill(step, False, True)
        send(step)
        return carry

    def both(step, carry):
        arrive(step - LAG)
        fill(step, True, True)
        send(step)
        return carry

    def reflected(step, carry):
        reflect(step).wait_recv()
        return carry

    load.wait()
    parts[0].wait_recv()
    for step in range(LAG):
        fill(step, True, False)
        send(step)
    parts[1].wait_recv()
    lax.fori_loop(LAG, SEQS - 1, both, 0)
    both(SEQS - 1, 0)
    lax.fori_loop(SEQS, EARLY + LAG + 3, pass_on, 0)
    parts[2].wait_recv()
    lax.fori_loop(0, EARLY + 1, reflected, 0)

    def local_rows(k, chunk, half):
        return jnp.where(root_core[k], own[chunk, half], other[chunk, half])

    for chunk in range(W // (2 * G)):
        step, t = chunk // LINKS, chunk % LINKS
        for half, got in ((core, recv), (1 - core, mirror)):
            value = got[step, 0, 0]
            for d in range(6):
                here = got[step + LAG * d, 0, 0]
                for m in range(1, LINKS):
                    here = jnp.where(entry[0][t] == m, got[step + LAG * d, m, 0], here)
                value = jnp.where(level[0][t] == d, here, value)
            q[0, chunk, half] = jnp.where(rooted[0], local_rows(0, chunk, half), value)

    def matrix(k, window):
        return q[k, window * G : (window + 1) * G].reshape(W, W)

    def turn(k, window):
        turned = matrix(k, window).T
        q[k, window * G : (window + 1) * G] = turned.reshape(G, 2, G, W)

    def product(left, right):
        return jnp.dot(left, right, preferred_element_type=jnp.float32).astype(jnp.bfloat16)

    def full(k, window, first):
        def panel(index, carry):
            columns = pl.ds(pl.multiple_of(index * 256, 256), 256)
            rows = pl.ds(first, W)
            w[rows, columns] = product(matrix(k, window), w[rows, columns])
            return carry

        lax.fori_loop(0, 4, panel, 0)

    def band(c):
        return pl.ds(c * BAND, BAND)

    def up(k, c):
        return pltpu.make_async_remote_copy(
            src_ref=w.at[pl.ds(0, EDGE), band(c)],
            dst_ref=below.at[k, :, band(c)],
            send_sem=up_send.at[k, c],
            recv_sem=up_recv.at[k, c],
            device_id=upper,
            device_id_type=MESH,
        )

    def down(k, c):
        return pltpu.make_async_remote_copy(
            src_ref=back.at[k, :, band(c)],
            dst_ref=top.at[k, :, band(c)],
            send_sem=down_send.at[k, c],
            recv_sem=down_recv.at[k, c],
            device_id=lower,
            device_id_type=MESH,
        )

    inner = row > 0
    outer = row < 3

    load_slab.wait()
    turn(0, 0)
    full(0, 0, 0)

    @pl.when(row == 0)
    def _():
        top[0] = w[0:EDGE, :]

    lax.fori_loop(EARLY + LAG + 3, STEPS, pass_on, 0)

    @pl.when(inner)
    def _():
        for c in range(BANDS):
            up(0, c).start()

    def drain(step, carry):
        arrive(step)
        return carry

    lax.fori_loop(STEPS - LAG, STEPS, drain, 0)
    lax.fori_loop(EARLY + 1, STEPS, reflected, 0)

    def place_chunk(k, t, step):
        chunk = step * LINKS + t
        index = level[k][t] * LAG + step
        for half, got in ((core, recv), (1 - core, mirror)):
            q[k, chunk, half] = jnp.where(
                rooted[k], local_rows(k, chunk, half), got[index, entry[k][t], k]
            )

    def gather(k, first):
        def body(step, carry):
            for t in range(LINKS):
                place_chunk(k, t, step)
            return carry

        lax.fori_loop(first, SEQS - 1, body, 0)
        for t in range(CHUNKS - LINKS * (SEQS - 1)):
            place_chunk(k, t, SEQS - 1)

    gather(0, 4)
    for t in range(1, LINKS):
        place_chunk(0, t, 3)
    for i in range(1, 8):
        turn(0, i)
    for i in range(1, 4):
        full(0, i, i * W)
    for i in range(3):
        full(0, 4 + i, EDGE + i * W)

    last = 2048 - EDGE

    def cross(k, c):
        @pl.when(outer)
        def _():
            up(k, c).wait_recv()
            pair = jnp.concatenate([w[last:, band(c)], below[k, :, band(c)]], 0)
            mixed = product(matrix(k, 7), pair)
            back[k, :, band(c)] = mixed[EDGE:]
            down(k, c).start()
            w[last:, band(c)] = mixed[:EDGE]

    def lowest(c):
        rows = pl.ds(3 * W, W)
        w[rows, band(c)] = product(matrix(1, 3), w[rows, band(c)])

    def first_again(c):
        @pl.when(inner)
        def _():
            up(0, c).wait_send()
            down(0, c).wait_recv()

        pair = jnp.concatenate([top[0, :, band(c)], w[EDGE:W, band(c)]], 0)
        w[0:W, band(c)] = product(matrix(1, 0), pair)

        @pl.when(inner)
        def _():
            up(1, c).start()

    def store(index, source, rows, columns):
        return pltpu.make_async_copy(source, out_hbm.at[rows, columns], out_sem.at[index])

    def store_last(c):
        return store(c, w.at[pl.ds(last, EDGE), band(c)], pl.ds(last, EDGE), band(c))

    def store_middle():
        rows = pl.ds(EDGE, last - EDGE)
        return pltpu.make_async_copy(w.at[rows], out_hbm.at[rows], out_sem.at[16])

    def store_first(c):
        return store(8 + c, top.at[1, :, band(c)], pl.ds(0, EDGE), band(c))

    def finish(c):
        @pl.when(inner)
        def _():
            down(1, c).wait_recv()

        @pl.when(row == 0)
        def _():
            top[1, :, band(c)] = w[0:EDGE, band(c)]

        store_first(c).start()

    for c in range(4):
        cross(0, c)
    gather(1, 0)
    for i in range(8):
        turn(1, i)
    for i in range(1, 3):
        full(1, i, i * W)
    for c in range(4):
        lowest(c)
    for c in range(2):
        first_again(c)
    for c in range(4, 8):
        cross(0, c)
        lowest(c)
        first_again(c - 2)
    first_again(6)
    cross(1, 0)
    store_last(0).start()
    first_again(7)
    for i in range(3):
        full(1, 4 + i, EDGE + i * W)
    store_middle().start()
    for c in range(1, 8):
        cross(1, c)
        store_last(c).start()
        if c >= 2:
            finish(c - 2)
    finish(6)
    finish(7)

    def settle(step, carry):
        reflect(step).wait_send()
        whole(stage, step, send_sem).wait()
        return carry

    lax.fori_loop(0, STEPS, settle, 0)
    for copy in parts:
        copy.wait_send()
    for c in range(BANDS):
        store_last(c).wait()
        store_first(c).wait()

        @pl.when(inner)
        def _(c=c):
            up(1, c).wait_send()

        @pl.when(outer)
        def _(c=c):
            down(0, c).wait_send()
            down(1, c).wait_send()

    store_middle().wait()


def local(slab, transforms, owners):
    half = (2, G, W)
    rows, columns = slab.shape
    dma = pltpu.SemaphoreType.DMA
    return pl.pallas_call(
        sweep_kernel,
        out_shape=jax.ShapeDtypeStruct(slab.shape, jnp.bfloat16),
        in_specs=[
            pl.BlockSpec(memory_space=pltpu.SMEM),
            pl.BlockSpec(memory_space=pltpu.SMEM),
            pl.BlockSpec(memory_space=pl.ANY),
            pl.BlockSpec(memory_space=pl.ANY),
        ],
        out_specs=pl.BlockSpec(memory_space=pl.ANY),
        scratch_shapes=[
            pltpu.VMEM((CHUNKS,) + half, jnp.bfloat16),
            pltpu.VMEM((CHUNKS,) + half, jnp.bfloat16),
            pltpu.VMEM((STEPS, LINKS) + half, jnp.bfloat16),
            pltpu.VMEM((STEPS, LINKS) + half, jnp.bfloat16),
            pltpu.VMEM((STEPS, LINKS) + half, jnp.bfloat16),
            pltpu.VMEM((2, CHUNKS) + half, jnp.bfloat16),
            pltpu.VMEM((rows, columns), jnp.bfloat16),
            pltpu.VMEM((2, EDGE, columns), jnp.bfloat16),
            pltpu.VMEM((2, EDGE, columns), jnp.bfloat16),
            pltpu.VMEM((2, EDGE, columns), jnp.bfloat16),
            dma((2,)),
            dma((3,)),
            dma((3,)),
            dma((STEPS,)),
            dma((STEPS,)),
            dma((STEPS,)),
            dma((STEPS,)),
            dma((2, BANDS)),
            dma((2, BANDS)),
            dma((2, BANDS)),
            dma((2, BANDS)),
            dma((2 * BANDS + 1,)),
        ],
        compiler_params=pltpu.CompilerParams(
            collective_id=0, has_side_effects=True, vmem_limit_bytes=62 * 1024 * 1024
        ),
        name="sweep",
    )(owners, tree_tables(), transforms[0].reshape((CHUNKS,) + half), slab)


def solution(mesh):
    return jax.shard_map(
        local,
        mesh=mesh,
        in_specs=(P("rows", "cols"), P("cols", "rows", None), P()),
        out_specs=P("rows", "cols"),
        check_vma=False,
    )
```

time: 693 us -> 126 us (0.18)
  the two profiles are of different devices: /device:TPU:126 before, /device:TPU:224 now
where the time goes in v1:
time: 126 us
  Pallas kernels  121 us (96%)
  local copies, waits for them, and re-layouts  4.64 us (4%)
    pallas_call x1, Pallas kernels, local(): pl.pallas_call(sweep_kernel, out_shape=jax.ShapeDtypeStruct(slab.shape, j...  121 us
    unnamed x1, local copies, waits for them, and re-layouts  4.64 us

profile of v1, /device:TPU:224, one launch (start us, length us, event | category | flops | bytes accessed | tf_op | source)
XLA Modules:
  0.0 125.8 jit_solution(1690471275553639160)
XLA Ops:
  0.0 121.2 %sweep.1 = bf16[2048,1024]{1,0:T(8,128)(2,1)} custom-call(s32[2,4]{1,0:T(2,128)} %owners.1, s32[480]{0:T(512)} %constant.2.clone.table, bf16[128,2,16,512]{3,2,1,0:T(8,128)(2,1)} %bitcast.1, bf16[2048,1024]{1,0:T(8,128)(2,1)} %slab_hbm.1), custom_call_target="tpu_custom_call" | custom-call | tf_op jit(solution)/shard_map/sweep/pallas_call | solution.py:426
  121.2 4.6 %copy.6 = bf16[2048,1024]{1,0:T(8,128)(2,1)} copy(bf16[2048,1024]{1,0:T(8,128)(2,1)} %sweep.1) | data formatting | bytes 8388608

commit v2 on v1

--- a/solution.py
+++ b/solution.py
@@ -67,10 +67,10 @@
 
 
 def sweep_kernel(
-    owners, table, slot_hbm, slab_hbm, out_hbm,
-    own, other, recv, mirror, stage, q, w, below, top, back,
+    owners, table, slot_hbm, slab_hbm, w,
+    own, other, recv, mirror, stage, q, below, top, back,
     load_sem, part_send, part_recv, send_sem, recv_sem, mirror_send, mirror_recv,
-    up_send, up_recv, down_send, down_recv, out_sem,
+    up_send, up_recv, down_send, down_recv,
 ):
     row = lax.axis_index("rows")
     col = lax.axis_index("cols")
@@ -93,10 +93,14 @@
     upper = {"rows": (row + 3) % 4}
     lower = {"rows": (row + 1) % 4}
 
-    load = pltpu.make_async_copy(slot_hbm, own, load_sem.at[0])
-    load.start()
-    load_slab = pltpu.make_async_copy(slab_hbm, w, load_sem.at[1])
-    load_slab.start()
+    def load(index, first, count):
+        rows = pl.ds(first, count)
+        return pltpu.make_async_copy(slot_hbm.at[rows], own.at[rows], load_sem.at[index])
+
+    loads = (load(0, 0, 32), load(1, 32, 96))
+    load_slab = pltpu.make_async_copy(slab_hbm, w, load_sem.at[2])
+    for copy in loads:
+        copy.start()
     barrier = pltpu.get_barrier_semaphore()
     for peer in peers + (partner, upper, lower):
         pl.semaphore_signal(barrier, inc=1, device_id=peer, device_id_type=MESH)
@@ -113,7 +117,7 @@
         )
 
     parts = (part(0, 0, 32, 1 - core), part(1, 32, 96, 1 - core), part(2, 0, 128, core))
-    for copy in parts:
+    for copy in parts[:2]:
         copy.start()
 
     place, rooted, root_core = [], [], []
@@ -191,12 +195,15 @@
         reflect(step).wait_recv()
         return carry
 
-    load.wait()
+    loads[0].wait()
     parts[0].wait_recv()
     for step in range(LAG):
         fill(step, True, False)
         send(step)
+    loads[1].wait()
     parts[1].wait_recv()
+    parts[2].start()
+    load_slab.start()
     lax.fori_loop(LAG, SEQS - 1, both, 0)
     both(SEQS - 1, 0)
     lax.fori_loop(SEQS, EARLY + LAG + 3, pass_on, 0)
@@ -228,13 +235,8 @@
         return jnp.dot(left, right, preferred_element_type=jnp.float32).astype(jnp.bfloat16)
 
     def full(k, window, first):
-        def panel(index, carry):
-            columns = pl.ds(pl.multiple_of(index * 256, 256), 256)
-            rows = pl.ds(first, W)
-            w[rows, columns] = product(matrix(k, window), w[rows, columns])
-            return carry
-
-        lax.fori_loop(0, 4, panel, 0)
+        rows = pl.ds(first, W)
+        w[rows, :] = product(matrix(k, window), w[rows, :])
 
     def band(c):
         return pl.ds(c * BAND, BAND)
@@ -324,9 +326,9 @@
             down(k, c).start()
             w[last:, band(c)] = mixed[:EDGE]
 
-    def lowest(c):
-        rows = pl.ds(3 * W, W)
-        w[rows, band(c)] = product(matrix(1, 3), w[rows, band(c)])
+    def lowest(first):
+        rows, columns = pl.ds(3 * W, W), pl.ds(first * BAND, 4 * BAND)
+        w[rows, columns] = product(matrix(1, 3), w[rows, columns])
 
     def first_again(c):
         @pl.when(inner)
@@ -341,57 +343,46 @@
         def _():
             up(1, c).start()
 
-    def store(index, source, rows, columns):
-        return pltpu.make_async_copy(source, out_hbm.at[rows, columns], out_sem.at[index])
-
-    def store_last(c):
-        return store(c, w.at[pl.ds(last, EDGE), band(c)], pl.ds(last, EDGE), band(c))
-
-    def store_middle():
-        rows = pl.ds(EDGE, last - EDGE)
-        return pltpu.make_async_copy(w.at[rows], out_hbm.at[rows], out_sem.at[16])
-
-    def store_first(c):
-        return store(8 + c, top.at[1, :, band(c)], pl.ds(0, EDGE), band(c))
-
     def finish(c):
         @pl.when(inner)
         def _():
+            up(1, c).wait_send()
             down(1, c).wait_recv()
-
-        @pl.when(row == 0)
-        def _():
-            top[1, :, band(c)] = w[0:EDGE, band(c)]
-
-        store_first(c).start()
-
-    for c in range(4):
+            w[0:EDGE, band(c)] = top[1, :, band(c)]
+
+    for c in range(3):
         cross(0, c)
     gather(1, 0)
-    for i in range(8):
+    turn(1, 0)
+    first_again(0)
+    cross(0, 3)
+    first_again(1)
+    for i in range(1, 4):
         turn(1, i)
-    for i in range(1, 3):
-        full(1, i, i * W)
-    for c in range(4):
-        lowest(c)
-    for c in range(2):
-        first_again(c)
-    for c in range(4, 8):
-        cross(0, c)
-        lowest(c)
-        first_again(c - 2)
+    lowest(0)
+    cross(0, 4)
+    first_again(2)
+    full(1, 1, W)
+    cross(0, 5)
+    first_again(3)
+    full(1, 2, 2 * W)
+    cross(0, 6)
+    first_again(4)
+    for i in range(4, 8):
+        turn(1, i)
+    cross(0, 7)
+    first_again(5)
+    lowest(4)
     first_again(6)
     cross(1, 0)
-    store_last(0).start()
     first_again(7)
     for i in range(3):
         full(1, 4 + i, EDGE + i * W)
-    store_middle().start()
     for c in range(1, 8):
         cross(1, c)
-        store_last(c).start()
-        if c >= 2:
-            finish(c - 2)
+        if c >= 3:
+            finish(c - 3)
+    finish(5)
     finish(6)
     finish(7)
 
@@ -404,19 +395,11 @@
     for copy in parts:
         copy.wait_send()
     for c in range(BANDS):
-        store_last(c).wait()
-        store_first(c).wait()
-
-        @pl.when(inner)
-        def _(c=c):
-            up(1, c).wait_send()
 
         @pl.when(outer)
         def _(c=c):
             down(0, c).wait_send()
             down(1, c).wait_send()
-
-    store_middle().wait()
 
 
 def local(slab, transforms, owners):
@@ -425,14 +408,14 @@
     dma = pltpu.SemaphoreType.DMA
     return pl.pallas_call(
         sweep_kernel,
-        out_shape=jax.ShapeDtypeStruct(slab.shape, jnp.bfloat16),
+        out_shape=pltpu.VMEM(slab.shape, jnp.bfloat16),
         in_specs=[
             pl.BlockSpec(memory_space=pltpu.SMEM),
             pl.BlockSpec(memory_space=pltpu.SMEM),
             pl.BlockSpec(memory_space=pl.ANY),
             pl.BlockSpec(memory_space=pl.ANY),
         ],
-        out_specs=pl.BlockSpec(memory_space=pl.ANY),
+        out_specs=pl.BlockSpec(memory_space=pltpu.VMEM),
         scratch_shapes=[
             pltpu.VMEM((CHUNKS,) + half, jnp.bfloat16),
             pltpu.VMEM((CHUNKS,) + half, jnp.bfloat16),
@@ -440,11 +423,10 @@
             pltpu.VMEM((STEPS, LINKS) + half, jnp.bfloat16),
             pltpu.VMEM((STEPS, LINKS) + half, jnp.bfloat16),
             pltpu.VMEM((2, CHUNKS) + half, jnp.bfloat16),
-            pltpu.VMEM((rows, columns), jnp.bfloat16),
             pltpu.VMEM((2, EDGE, columns), jnp.bfloat16),
             pltpu.VMEM((2, EDGE, columns), jnp.bfloat16),
             pltpu.VMEM((2, EDGE, columns), jnp.bfloat16),
-            dma((2,)),
+            dma((3,)),
             dma((3,)),
             dma((3,)),
             dma((STEPS,)),
@@ -455,10 +437,9 @@
             dma((2, BANDS)),
             dma((2, BANDS)),
             dma((2, BANDS)),
-            dma((2 * BANDS + 1,)),
         ],
         compiler_params=pltpu.CompilerParams(
-            collective_id=0, has_side_effects=True, vmem_limit_bytes=62 * 1024 * 1024
+            collective_id=0, has_side_effects=True, vmem_limit_bytes=56 * 1024 * 1024
         ),
         name="sweep",
     )(owners, tree_tables(), transforms[0].reshape((CHUNKS,) + half), slab)

time: 126 us -> 114 us (0.905)
  Pallas kernels: 121 us -> 111 us
  local copies, waits for them, and re-layouts: 4.64 us -> 2.02 us
    pallas_call x1, Pallas kernels: 121 us -> 111 us  [local(): pl.pallas_call(sweep_kernel, out_shape=pltpu.VMEM(slab.shape, jnp.bfloat1...]
    unnamed x1, local copies, waits for them, and re-layouts: 4.64 us -> 2.02 us
where the time goes in v2:
time: 114 us; the launch traced here: 113 us
  Pallas kernels  111 us (97%)
  local copies, waits for them, and re-layouts  2.02 us (2%)
    pallas_call x1, Pallas kernels, local(): pl.pallas_call(sweep_kernel, out_shape=pltpu.VMEM(slab.shape, jnp.bfloat1...  111 us

profile of v2, /device:TPU:224, one launch (start us, length us, event | category | flops | bytes accessed | tf_op | source)
XLA Modules:
  0.0 113.2 jit_solution(5118135247884751778)
XLA Ops:
  0.0 111.2 %sweep.1 = bf16[2048,1024]{1,0:T(8,128)(2,1)S(1)} custom-call(s32[2,4]{1,0:T(2,128)} %owners.1, s32[480]{0:T(512)} %constant.2.clone.table, bf16[128,2,16,512]{3,2,1,0:T(8,128)(2,1)} %bitcast.1, bf16[2048,1024]{1,0:T(8,128)(2,1)} %slab_hbm.1), custom_call_target="tpu_custom_call" | custom-call | tf_op jit(solution)/shard_map/sweep/pallas_call | solution.py:409
  111.2 2.0 %copy.6 = bf16[2048,1024]{1,0:T(8,128)(2,1)} copy(bf16[2048,1024]{1,0:T(8,128)(2,1)S(1)} %sweep.1) | data formatting | bytes 8388608

commit v3 on v2

--- a/solution.py
+++ b/solution.py
@@ -66,6 +66,19 @@
     return jnp.array(flat, jnp.int32)
 
 
+def reach():
+    parent, depth = digits(PARENT), digits(DEPTH)
+    trees = []
+    for t in range(LINKS):
+        seen = {(depth[p][t] - 1, parent[p][t]) for p in range(1, 32)}
+        levels = sorted({d for d, _ in seen})
+        trees.append([(d, sorted(m for e, m in seen if e == d)) for d in levels])
+    return trees
+
+
+REACH = reach()
+
+
 def sweep_kernel(
     owners, table, slot_hbm, slab_hbm, w,
     own, other, recv, mirror, stage, q, below, top, back,
@@ -216,12 +229,12 @@
     for chunk in range(W // (2 * G)):
         step, t = chunk // LINKS, chunk % LINKS
         for half, got in ((core, recv), (1 - core, mirror)):
-            value = got[step, 0, 0]
-            for d in range(6):
-                here = got[step + LAG * d, 0, 0]
-                for m in range(1, LINKS):
+            value = None
+            for d, links in REACH[t]:
+                here = got[step + LAG * d, links[0], 0]
+                for m in links[1:]:
                     here = jnp.where(entry[0][t] == m, got[step + LAG * d, m, 0], here)
-                value = jnp.where(level[0][t] == d, here, value)
+                value = here if value is None else jnp.where(level[0][t] == d, here, value)
             q[0, chunk, half] = jnp.where(rooted[0], local_rows(0, chunk, half), value)
 
     def matrix(k, window):
@@ -274,16 +287,18 @@
 
     lax.fori_loop(EARLY + LAG + 3, STEPS, pass_on, 0)
 
+
+    def drain(step, carry):
+        arrive(step)
+        return carry
+
+    lax.fori_loop(STEPS - LAG, STEPS, drain, 0)
+
     @pl.when(inner)
     def _():
         for c in range(BANDS):
             up(0, c).start()
 
-    def drain(step, carry):
-        arrive(step)
-        return carry
-
-    lax.fori_loop(STEPS - LAG, STEPS, drain, 0)
     lax.fori_loop(EARLY + 1, STEPS, reflected, 0)
 
     def place_chunk(k, t, step):

time: 114 us -> 111 us (0.974)
  the two profiles are of different devices: /device:TPU:224 before, /device:TPU:192 now
where the time goes in v3:
time: 111 us
  Pallas kernels  109 us (98%)
  local copies, waits for them, and re-layouts  2.02 us (2%)
    pallas_call x1, Pallas kernels, local(): pl.pallas_call(sweep_kernel, out_shape=pltpu.VMEM(slab.shape, jnp.bfloat1...  109 us

profile of v3, /device:TPU:192, one launch (start us, length us, event | category | flops | bytes accessed | tf_op | source)
XLA Modules:
  0.0 111.0 jit_solution(587957616913984435)
XLA Ops:
  0.0 108.9 %sweep.1 = bf16[2048,1024]{1,0:T(8,128)(2,1)S(1)} custom-call(s32[2,4]{1,0:T(2,128)} %owners.1, s32[480]{0:T(512)} %constant.2.clone.table, bf16[128,2,16,512]{3,2,1,0:T(8,128)(2,1)} %bitcast.1, bf16[2048,1024]{1,0:T(8,128)(2,1)} %slab_hbm.1), custom_call_target="tpu_custom_call" | custom-call | tf_op jit(solution)/shard_map/sweep/pallas_call | solution.py:424
  108.9 2.0 %copy.6 = bf16[2048,1024]{1,0:T(8,128)(2,1)} copy(bf16[2048,1024]{1,0:T(8,128)(2,1)S(1)} %sweep.1) | data formatting | bytes 8388608
